TPU v7x, 512 devices: a whole 4x8x8 slice. The times are simulated.
512 devices in a mesh: layer: 2 (over core), row: 16 (over x, z_hi), col: 16 (over z_lo, y).
Axes of the slice: x: 4, y: 8, z: 8 (z_hi: 4, z_lo: 2; z = z_hi * 2 + z_lo), core: 2. Of those that a mesh axis runs over, the one named last changes fastest.
Arguments:
- rhs_sub: float32 [2, 3, 1, 16, 256, 512], P('layer', None, None, 'row', 'col'), may hold values from -6 to 6
- rhs_top: float32 [1, 16, 256, 512], P(None, 'row', 'col'), may hold values from -6 to 6
- lower_inv_sub: float32 [2, 3, 1, 16, 256, 256], P('layer', None, None, 'row', 'col'), as said below
- lower_inv_top: float32 [1, 16, 256, 256], P(None, 'row', 'col'), as said below
- upper_inv_sub: float32 [2, 3, 1, 16, 256, 256], P('layer', None, None, 'row', 'col'), as said below
- upper_inv_top: float32 [1, 16, 256, 256], P(None, 'row', 'col'), as said below
- lower_sub: float32 [2, 3, 1, 16, 1, 16, 256, 256], P('layer', None, None, 'row', None, 'col'), may hold values from -0.09375 to 0.09375
- lower_top: float32 [2, 3, 1, 16, 1, 16, 256, 256], P('layer', None, None, 'row', None, 'col'), may hold values from -0.0546875 to 0.0546875
- upper_sub: float32 [2, 3, 1, 16, 1, 16, 256, 256], P('layer', None, None, 'row', None, 'col'), may hold values from -0.0625 to 0.0625
- upper_top: float32 [2, 3, 1, 16, 1, 16, 256, 256], P('layer', None, None, 'row', None, 'col'), may hold values from -0.09375 to 0.09375
- block_pattern: int32 [2, 4, 3, 1, 16, 1, 16], P('layer', None, None, None, 'row', None, 'col'), may hold values 0 or 1
Outputs:
- solution_sub: float32 [2, 3, 1, 16, 256, 512], P('layer', None, None, 'row', 'col')
- solution_top: float32 [1, 16, 256, 512], P(None, 'row', 'col')
Inputs may be any that keep to these rules, and one draw needn't show every extreme that they name: `lower_inv_sub`: every 256 x 256 block is lower triangular with unit diagonal. `lower_inv_top`: every 256 x 256 block is lower triangular with unit diagonal. `upper_inv_sub`: every 256 x 256 block is upper triangular with unit diagonal. `upper_inv_top`: every 256 x 256 block is upper triangular with unit diagonal.
All inputs are finite; a program needn't handle non-finite values. No bound on the sum of `block_pattern` on one device may be relied on, other than what follows from the above.
Results may differ from a plain program's by a relative error of at most 0.00014.
Values sent between devices are 32-bit elements; how exact they have to be, the bound alone decides.
No kernel may reach another device: no remote copies, remote signals or barrier semaphores. Data moves between devices by JAX's collectives and lax.ppermute only.
A program may use at most 64 MiB of HBM per device.

v0:
```python
import jax
import jax.numpy as jnp
from jax import lax
from jax.sharding import PartitionSpec as P

HIGHEST = lax.Precision.HIGHEST


def broadcast(x, axis, root):
    mine = lax.axis_index(axis) == root
    return lax.psum(jnp.where(mine, x, jnp.zeros_like(x)), axis)


def couple(blocks, pattern, solution):
    weighted = solution[None] * pattern[:, :, None, None].astype(jnp.float32)
    return jnp.einsum("tsab,tsbn->tan", blocks, weighted, precision=HIGHEST)


def spread(whole_block):
    return broadcast(whole_block, "row", lax.axis_index("col"))


def on_device(
    rhs_sub,
    rhs_top,
    lower_inv_sub,
    lower_inv_top,
    upper_inv_sub,
    upper_inv_top,
    lower_sub,
    lower_top,
    upper_sub,
    upper_top,
    block_pattern,
):
    lower_list = [lower_inv_sub[0, level, :, 0] for level in range(3)] + [lower_inv_top[:, 0]]
    upper_list = [upper_inv_sub[0, level, :, 0] for level in range(3)] + [upper_inv_top[:, 0]]
    right_sides = [rhs_sub[0, level, :, 0] for level in range(3)] + [rhs_top[:, 0]]

    def solve(partial_value, right_side, inverse_rows, top):
        if partial_value is None:
            residual = right_side
        else:
            share = lax.psum_scatter(partial_value, "col", scatter_dimension=1, tiled=True)
            if top:
                share = lax.psum(share, "layer")
            residual = right_side - share
        return jnp.einsum(
            "kab,kbn->kan",
            inverse_rows,
            lax.all_gather(residual, "col", axis=1, tiled=True),
            precision=HIGHEST,
        )

    def copy_out(solution):
        return spread(lax.all_gather(solution, "col", axis=1, tiled=True))

    def blocks(array, pair):
        return array[0, pair, :, 0, :, 0]

    def pattern(kind, pair):
        return block_pattern[0, kind, pair, :, 0, :, 0]

    fore_zero = solve(None, right_sides[0], lower_list[0], False)
    copy_zero = copy_out(fore_zero)
    into_one = couple(blocks(lower_sub, 0), pattern(0, 0), copy_zero)
    into_two = couple(blocks(lower_sub, 1), pattern(0, 1), copy_zero)
    into_top = couple(blocks(lower_top, 0), pattern(1, 0), copy_zero)
    fore_one = solve(into_one, right_sides[1], lower_list[1], False)
    copy_one = copy_out(fore_one)
    into_two = into_two + couple(blocks(lower_sub, 2), pattern(0, 2), copy_one)
    into_top = into_top + couple(blocks(lower_top, 1), pattern(1, 1), copy_one)
    fore_two = solve(into_two, right_sides[2], lower_list[2], False)
    copy_two = copy_out(fore_two)
    into_top = into_top + couple(blocks(lower_top, 2), pattern(1, 2), copy_two)
    fore_top = solve(into_top, right_sides[3], lower_list[3], True)
    final_top = solve(None, fore_top, upper_list[3], False)
    down_top = copy_out(final_top)
    toward_two = couple(blocks(upper_top, 2), pattern(3, 2), down_top)
    toward_one = couple(blocks(upper_top, 1), pattern(3, 1), down_top)
    toward_zero = couple(blocks(upper_top, 0), pattern(3, 0), down_top)
    final_two = solve(toward_two, fore_two, upper_list[2], False)
    down_two = copy_out(final_two)
    toward_one = toward_one + couple(blocks(upper_sub, 2), pattern(2, 2), down_two)
    toward_zero = toward_zero + couple(blocks(upper_sub, 1), pattern(2, 1), down_two)
    final_one = solve(toward_one, fore_one, upper_list[1], False)
    down_one = copy_out(final_one)
    toward_zero = toward_zero + couple(blocks(upper_sub, 0), pattern(2, 0), down_one)
    final_zero = solve(toward_zero, fore_zero, upper_list[0], False)
    solution_sub = jnp.stack([final_zero, final_one, final_two])[None, :, :, None]
    solution_top = final_top[:, None]
    return (solution_sub, solution_top)


def solution(mesh):
    placed = (
        P("layer", None, None, "row", "col", None),
        P(None, "row", "col", None),
        P("layer", None, None, "row", "col", None),
        P(None, "row", "col", None),
        P("layer", None, None, "row", "col", None),
        P(None, "row", "col", None),
        P("layer", None, None, "row", None, "col", None, None),
        P("layer", None, None, "row", None, "col", None, None),
        P("layer", None, None, "row", None, "col", None, None),
        P("layer", None, None, "row", None, "col", None, None),
        P("layer", None, None, None, "row", None, "col"),
    )
    return jax.shard_map(
        on_device,
        mesh=mesh,
        in_specs=placed,
        out_specs=(P("layer", None, None, "row", "col", None), P(None, "row", "col", None)),
        check_vma=False,
    )
```

profile of v0, /device:TPU:2, one launch (start us, length us, event | category | flops | bytes accessed | tf_op | source)
XLA Modules:
  0.0 2184.0 jit_solution(2908091870607377560)
XLA Ops:
  8.0 37.7 %all-gather = f32[1,1,1,1,256,512]{5,4,3,2,1,0:T(8,128)S(1)} all-gather(f32[1,1,1,1,16,512]{5,4,3,2,1,0:T(8,128)S(1)} %get-tuple-element.8), channel_id=2, replica_groups=mesh['layer'=2,'row'=16,'col'=16] {'col'}, dimensions={4}, use_global_device_ids=true | all-gather | bytes 557056 | tf_op jit(solution)/shard_map/all_gather | solution.py:51
  46.1 32.3 %all-gather.1 = f32[256,512]{1,0:T(8,128)S(1)} all-gather(f32[16,512]{1,0:T(8,128)S(1)} %fusion.33), channel_id=3, replica_groups=mesh['layer'=2,'row'=16,'col'=16] {'col'}, dimensions={0}, use_global_device_ids=true | all-gather | bytes 557056 | tf_op jit(solution)/shard_map/all_gather | solution.py:56
  81.3 168.6 %all-reduce.13.cloned.1.call-done = f32[1,256,512]{2,1,0:T(8,128)} async-done(((f32[1,256,512]{2,1,0:T(8,128)}), f32[1,256,512]{2,1,0:T(8,128)}) %all-reduce.13.cloned.1.call-update) | async-done | bytes 524304 | tf_op jit(solution)/shard_map/psum | solution.py:11
  255.0 140.9 %all-reduce.25.cloned.1.call-done = f32[1,256,512]{2,0,1:T(1,128)} async-done(((f32[1,256,512]{2,0,1:T(1,128)}), f32[1,256,512]{2,0,1:T(1,128)}) %all-reduce.25.cloned.1.call-update) | async-done | bytes 524304
  396.7 35.3 %all_gather.44 = f32[1,256,512]{2,0,1:T(1,128)S(1)} all-gather(f32[1,16,512]{2,0,1:T(1,128)S(1)} %fusion.84), channel_id=1, replica_groups=mesh['layer'=2,'row'=16,'col'=16] {'col'}, dimensions={1}, use_global_device_ids=true | all-gather | bytes 557056 | tf_op jit(solution)/shard_map/all_gather | solution.py:51
  468.0 165.1 %all-reduce.15.cloned.1.call-done = f32[1,256,512]{2,1,0:T(8,128)} async-done(((f32[1,256,512]{2,1,0:T(8,128)}), f32[1,256,512]{2,1,0:T(8,128)}) %all-reduce.15.cloned.1.call-update) | async-done | bytes 524304 | tf_op jit(solution)/shard_map/psum | solution.py:11
  638.1 141.0 %all-reduce.27.cloned.1.call-done = f32[1,256,512]{2,0,1:T(1,128)} async-done(((f32[1,256,512]{2,0,1:T(1,128)}), f32[1,256,512]{2,0,1:T(1,128)}) %all-reduce.27.cloned.1.call-update) | async-done | bytes 524304
  779.9 35.3 %all_gather.46 = f32[1,256,512]{2,0,1:T(1,128)S(1)} all-gather(f32[1,16,512]{2,0,1:T(1,128)S(1)} %fusion.83), channel_id=1, replica_groups=mesh['layer'=2,'row'=16,'col'=16] {'col'}, dimensions={1}, use_global_device_ids=true | all-gather | bytes 557056 | tf_op jit(solution)/shard_map/all_gather | solution.py:51
  851.3 165.0 %all-reduce.17.cloned.1.call-done = f32[1,256,512]{2,1,0:T(8,128)} async-done(((f32[1,256,512]{2,1,0:T(8,128)}), f32[1,256,512]{2,1,0:T(8,128)}) %all-reduce.17.cloned.1.call-update) | async-done | bytes 524304 | tf_op jit(solution)/shard_map/psum | solution.py:11
  1019.5 142.8 %all-reduce.29.cloned.1.call-done = f32[1,256,512]{2,0,1:T(1,128)} async-done(((f32[1,256,512]{2,0,1:T(1,128)}), f32[1,256,512]{2,0,1:T(1,128)}) %all-reduce.29.cloned.1.call-update) | async-done | bytes 524304
  1166.7 35.3 %all_gather.48 = f32[1,256,512]{2,0,1:T(1,128)S(1)} all-gather(f32[1,16,512]{2,0,1:T(1,128)S(1)} %reshape_subtract_fusion), channel_id=1, replica_groups=mesh['layer'=2,'row'=16,'col'=16] {'col'}, dimensions={1}, use_global_device_ids=true | all-gather | bytes 557056 | tf_op jit(solution)/shard_map/all_gather | solution.py:51
  1202.3 32.8 %all-gather.4 = f32[256,512]{1,0:T(8,128)S(1)} all-gather(f32[16,512]{1,0:T(8,128)S(1)} %convolution_bitcast_fusion.3), channel_id=6, replica_groups=mesh['layer'=2,'row'=16,'col'=16] {'col'}, dimensions={0}, use_global_device_ids=true | all-gather | bytes 557056 | tf_op jit(solution)/shard_map/all_gather | solution.py:51
  1235.5 34.6 %all-gather.5 = f32[256,512]{1,0:T(8,128)S(1)} all-gather(f32[16,512]{1,0:T(8,128)S(1)} %bitcast.211), channel_id=7, replica_groups=mesh['layer'=2,'row'=16,'col'=16] {'col'}, dimensions={0}, use_global_device_ids=true | all-gather | bytes 557056 | tf_op jit(solution)/shard_map/all_gather | solution.py:56
  1271.6 165.4 %all-reduce.19.cloned.1.call-done = f32[1,256,512]{2,1,0:T(8,128)} async-done(((f32[1,256,512]{2,1,0:T(8,128)}), f32[1,256,512]{2,1,0:T(8,128)}) %all-reduce.19.cloned.1.call-update) | async-done | bytes 524304 | tf_op jit(solution)/shard_map/psum | solution.py:11
  1439.5 75.0 %reduce-scatter.4.cloned.1.call-done = f32[1,16,512]{2,1,0:T(8,128)} async-done(((f32[1,256,512]{2,1,0:T(8,128)}), f32[1,16,512]{2,1,0:T(8,128)}) %reduce-scatter.4.cloned.1.call-update) | async-done | bytes 32784 | tf_op jit(solution)/shard_map/reduce_scatter | solution.py:44
  1515.3 33.9 %all_gather.51 = f32[1,256,512]{2,1,0:T(8,128)S(1)} all-gather(f32[1,16,512]{2,1,0:T(8,128)S(1)} %bitcast_subtract_fusion.1), channel_id=1, replica_groups=mesh['layer'=2,'row'=16,'col'=16] {'col'}, dimensions={1}, use_global_device_ids=true | all-gather | bytes 557056 | tf_op jit(solution)/shard_map/all_gather | solution.py:51
  1549.6 33.3 %all-gather.6 = f32[256,512]{1,0:T(8,128)S(1)} all-gather(f32[16,512]{1,0:T(8,128)S(1)} %bitcast.207), channel_id=8, replica_groups=mesh['layer'=2,'row'=16,'col'=16] {'col'}, dimensions={0}, use_global_device_ids=true | all-gather | bytes 557056 | tf_op jit(solution)/shard_map/all_gather | solution.py:56
  1586.2 164.1 %all-reduce.21.cloned.1.call-done = f32[1,256,512]{2,1,0:T(8,128)} async-done(((f32[1,256,512]{2,1,0:T(8,128)}), f32[1,256,512]{2,1,0:T(8,128)}) %all-reduce.21.cloned.1.call-update) | async-done | bytes 524304 | tf_op jit(solution)/shard_map/psum | solution.py:11
  1754.8 73.1 %reduce-scatter.6.cloned.1.call-done = f32[1,16,512]{2,1,0:T(8,128)} async-done(((f32[1,256,512]{2,1,0:T(8,128)}), f32[1,16,512]{2,1,0:T(8,128)}) %reduce-scatter.6.cloned.1.call-update) | async-done | bytes 32784 | tf_op jit(solution)/shard_map/reduce_scatter | solution.py:44
  1828.6 33.8 %all_gather.53 = f32[1,256,512]{2,1,0:T(8,128)S(1)} all-gather(f32[1,16,512]{2,1,0:T(8,128)S(1)} %bitcast_subtract_fusion), channel_id=1, replica_groups=mesh['layer'=2,'row'=16,'col'=16] {'col'}, dimensions={1}, use_global_device_ids=true | all-gather | bytes 557056 | tf_op jit(solution)/shard_map/all_gather | solution.py:51
  1862.8 33.3 %all-gather.7 = f32[256,512]{1,0:T(8,128)S(1)} all-gather(f32[16,512]{1,0:T(8,128)S(1)} %bitcast.209), channel_id=9, replica_groups=mesh['layer'=2,'row'=16,'col'=16] {'col'}, dimensions={0}, use_global_device_ids=true | all-gather | bytes 557056 | tf_op jit(solution)/shard_map/all_gather | solution.py:56
  1898.8 165.3 %all-reduce.23.cloned.1.call-done = f32[1,256,512]{2,1,0:T(8,128)} async-done(((f32[1,256,512]{2,1,0:T(8,128)}), f32[1,256,512]{2,1,0:T(8,128)}) %all-reduce.23.cloned.1.call-update) | async-done | bytes 524304 | tf_op jit(solution)/shard_map/psum | solution.py:11
  2066.6 75.0 %reduce-scatter.8.cloned.1.call-done = f32[1,16,512]{2,1,0:T(8,128)} async-done(((f32[1,256,512]{2,1,0:T(8,128)}), f32[1,16,512]{2,1,0:T(8,128)}) %reduce-scatter.8.cloned.1.call-update) | async-done | bytes 32784 | tf_op jit(solution)/shard_map/reduce_scatter | solution.py:44
  2142.4 33.8 %all_gather.55 = f32[1,256,512]{2,1,0:T(8,128)S(1)} all-gather(f32[1,16,512]{2,1,0:T(8,128)S(1)} %bitcast_subtract_fusion.2), channel_id=1, replica_groups=mesh['layer'=2,'row'=16,'col'=16] {'col'}, dimensions={1}, use_global_device_ids=true | all-gather | bytes 557056 | tf_op jit(solution)/shard_map/all_gather | solution.py:51
  (97 shorter events, 108.6 us)
Async XLA Ops:
  7.2 1194.8 %copy-start = (f32[1,1,16,256]{3,2,1,0:T(8,128)S(1)}, f32[1,1,16,256]{3,2,1,0:T(8,128)}, u32[]{:S(2)}) copy-start(f32[1,1,16,256]{3,2,1,0:T(8,128)} %param.14) | copy-start | bytes 49156
  7.2 242.7 %all-reduce.13.cloned.1.call-start = ((), (), s32[]{:S(2)}) async-start(), calls=%async_computation.3 | async-start | bytes 1048576 | tf_op jit(solution)/shard_map/psum | solution.py:11
  8.0 37.7 %copy-start.10 = (f32[1,3,1,1,16,256]{5,4,3,2,1,0:T(8,128)S(1)}, f32[1,3,1,1,16,256]{5,4,3,2,1,0:T(8,128)}, u32[]{:S(2)}) copy-start(f32[1,3,1,1,16,256]{5,4,3,2,1,0:T(8,128)} %param.13) | copy-start | bytes 147460
  78.4 171.5 %copy-start.6 = (f32[1,3,1,1,1,1,256,256]{7,6,5,4,3,2,1,0:T(8,128)S(1)}, f32[1,3,1,1,1,1,256,256]{7,6,5,4,3,2,1,0:T(8,128)}, u32[]{:S(2)}) copy-start(f32[1,3,1,1,1,1,256,256]{7,6,5,4,3,2,1,0:T(8,128)} %param.17) | copy-start | bytes 2359300
  79.3 316.6 %all-reduce.25.cloned.1.call-start = ((), (), s32[]{:S(2)}) async-start(), calls=%async_computation.12 | async-start | bytes 1048576
  253.0 380.1 %all-reduce.15.cloned.1.call-start = ((), (), s32[]{:S(2)}) async-start(), calls=%async_computation.4 | async-start | bytes 1048576 | tf_op jit(solution)/shard_map/psum | solution.py:11
  465.6 1.4 copy-start.1
  465.6 313.5 %all-reduce.27.cloned.1.call-start = ((), (), s32[]{:S(2)}) async-start(), calls=%async_computation.13 | async-start | bytes 1048576
  636.2 380.1 %all-reduce.17.cloned.1.call-start = ((), (), s32[]{:S(2)}) async-start(), calls=%async_computation.5 | async-start | bytes 1048576 | tf_op jit(solution)/shard_map/psum | solution.py:11
  847.9 1.3 copy-start.7
  848.8 313.5 %all-reduce.29.cloned.1.call-start = ((), (), s32[]{:S(2)}) async-start(), calls=%async_computation.14 | async-start | bytes 1048576
  1019.4 417.5 %all-reduce.19.cloned.1.call-start = ((), (), s32[]{:S(2)}) async-start(), calls=%async_computation.6 | async-start | bytes 1048576 | tf_op jit(solution)/shard_map/psum | solution.py:11
  1163.1 3.5 copy-start.12
  1202.3 32.8 %copy-start.14 = (f32[1,1,16,256]{3,2,1,0:T(8,128)S(1)}, f32[1,1,16,256]{3,2,1,0:T(8,128)}, u32[]{:S(2)}) copy-start(f32[1,1,16,256]{3,2,1,0:T(8,128)} %param.16) | copy-start | bytes 49156
  1235.5 34.6 %copy-start.9 = (f32[512,16]{0,1:T(8,128)}, f32[512,16]{0,1:T(8,128)S(1)}, u32[]{:S(2)}) copy-start(f32[512,16]{0,1:T(8,128)S(1)} %fusion.88) | copy-start | bytes 98308
  1270.0 166.9 %copy-start.5 = (f32[1,3,1,1,1,1,256,256]{7,6,5,4,3,2,1,0:T(8,128)S(1)}, f32[1,3,1,1,1,1,256,256]{7,6,5,4,3,2,1,0:T(8,128)}, u32[]{:S(2)}) copy-start(f32[1,3,1,1,1,1,256,256]{7,6,5,4,3,2,1,0:T(8,128)} %param.20) | copy-start | bytes 2359300
  1270.9 243.7 %reduce-scatter.4.cloned.1.call-start = ((), (), s32[]{:S(2)}) async-start(), calls=%async_computation.7 | async-start | bytes 557056 | tf_op jit(solution)/shard_map/reduce_scatter | solution.py:44
  1439.5 310.9 %all-reduce.21.cloned.1.call-start = ((), (), s32[]{:S(2)}) async-start(), calls=%async_computation.8 | async-start | bytes 1048576 | tf_op jit(solution)/shard_map/psum | solution.py:11
  1515.3 33.9 %copy-start.11 = (f32[1,3,1,1,16,256]{5,4,3,2,1,0:T(8,128)S(1)}, f32[1,3,1,1,16,256]{5,4,3,2,1,0:T(8,128)}, u32[]{:S(2)}) copy-start(f32[1,3,1,1,16,256]{5,4,3,2,1,0:T(8,128)} %param.15) | copy-start | bytes 147460
  1583.8 1.8 copy-start.2
  1583.8 166.6 %copy-start.8 = (f32[1,3,1,1,1,1,256,256]{7,6,5,4,3,2,1,0:T(8,128)S(1)}, f32[1,3,1,1,1,1,256,256]{7,6,5,4,3,2,1,0:T(8,128)}, u32[]{:S(2)}) copy-start(f32[1,3,1,1,1,1,256,256]{7,6,5,4,3,2,1,0:T(8,128)} %param.19) | copy-start | bytes 2359300
  1583.8 244.0 %reduce-scatter.6.cloned.1.call-start = ((), (), s32[]{:S(2)}) async-start(), calls=%async_computation.9 | async-start | bytes 557056 | tf_op jit(solution)/shard_map/reduce_scatter | solution.py:44
  1752.9 311.2 %all-reduce.23.cloned.1.call-start = ((), (), s32[]{:S(2)}) async-start(), calls=%async_computation.10 | async-start | bytes 1048576 | tf_op jit(solution)/shard_map/psum | solution.py:11
  1897.0 244.6 %reduce-scatter.8.cloned.1.call-start = ((), (), s32[]{:S(2)}) async-start(), calls=%async_computation.11 | async-start | bytes 557056 | tf_op jit(solution)/shard_map/reduce_scatter | solution.py:44
  (3 other events, 2.8 us)
Sparse Core Ops, SparseCore 0:
  79.4 170.4 all-reduce.12
  253.1 142.7 all-reduce.24
  465.8 167.2 all-reduce.14
  636.3 142.7 all-reduce.26
  849.0 167.2 all-reduce.16
  1019.6 142.7 all-reduce.28
  1271.0 165.8 all-reduce.18
  1439.7 74.7 reduce-scatter.3
  1583.9 166.4 all-reduce.20
  1753.0 74.7 reduce-scatter.5
  1897.1 166.9 all-reduce.22
  2066.8 74.7 reduce-scatter.7
where the time goes:
time: 2190 us; the launch traced here: 2180 us
  waiting for transfers between devices  1640 us (75%)
  blocking collectives  479 us (22%)
  between operations  22.8 us (1%)
    psum x6, waiting for transfers between devices, broadcast(): return lax.psum(jnp.where(mine, x, jnp.zeros_like(x)), axis)  994 us
    unnamed x15, waiting for transfers between devices  425 us
    all_gather x8, blocking collectives, solve(): lax.all_gather(residual, 'col', axis=1, tiled=True)  278 us
    reduce_scatter x3, waiting for transfers between devices, solve(): lax.psum_scatter(partial_value, 'col', scatter_dimension=1, tiled=True)  223 us
    all_gather x6, blocking collectives, copy_out(): return spread(lax.all_gather(solution, 'col', axis=1, tiled=True))  198 us
  transfers between devices with their start and end apart: 12, of which 12 were waited for; matrix products, arithmetic and copies ran while one was open for 0% of the time, Pallas kernels for 0%

commit v1 on v0

--- a/solution.py
+++ b/solution.py
@@ -8,7 +8,7 @@
 
 def broadcast(x, axis, root):
     mine = lax.axis_index(axis) == root
-    return lax.psum(jnp.where(mine, x, jnp.zeros_like(x)), axis)
+    return jnp.sum(lax.all_gather(jnp.where(mine, x, jnp.zeros_like(x)), axis), axis=0)
 
 
 def couple(blocks, pattern, solution):

time: 2190 us -> 1900 us (0.87)
  waiting for transfers between devices: 1640 us -> 1340 us
  other arithmetic: 9.74 us -> 36.2 us
    psum x6 -> x0, waiting for transfers between devices: 994 us -> none  [broadcast(): return lax.psum(jnp.where(mine, x, jnp.zeros_like(x)), axis)]
    all_gather x0 -> x6, waiting for transfers between devices: none -> 707 us  [broadcast(): lax.all_gather(jnp.where(mine, x, jnp.zeros_like(x)), axis)]
    reduce_sum x0 -> x6, other arithmetic: none -> 26.4 us  [broadcast(): jnp.sum(lax.all_gather(jnp.where(mine, x, jnp.zeros_like(x)), axis), axis=0)]
  transfers between devices with their start and end apart: 12 -> 12, of which waited for: 12 -> 12; matrix products, arithmetic and copies ran while one was open for 0% -> 1% of each run, Pallas kernels for 0% -> 0%
where the time goes in v1:
time: 1900 us
  waiting for transfers between devices  1340 us (71%)
  blocking collectives  479 us (25%)
  other arithmetic  36.2 us (2%)
  between operations  22.4 us (1%)
  matrix products  19.2 us (1%)
    all_gather x6, waiting for transfers between devices, broadcast(): lax.all_gather(jnp.where(mine, x, jnp.zeros_like(x)), axis)  707 us
    unnamed x15, waiting for transfers between devices  416 us
    all_gather x8, blocking collectives, solve(): lax.all_gather(residual, 'col', axis=1, tiled=True)  278 us
    reduce_scatter x3, waiting for transfers between devices, solve(): lax.psum_scatter(partial_value, 'col', scatter_dimension=1, tiled=True)  214 us
    all_gather x6, blocking collectives, copy_out(): return spread(lax.all_gather(solution, 'col', axis=1, tiled=True))  197 us
  transfers between devices with their start and end apart: 12, of which 12 were waited for; matrix products, arithmetic and copies ran while one was open for 1% of the time, Pallas kernels for 0%

profile of v1, /device:TPU:2, one launch (start us, length us, event | category | flops | bytes accessed | tf_op | source)
XLA Modules:
  0.0 1903.0 jit_solution(3905579566187182447)
XLA Ops:
  8.1 37.8 %all-gather = f32[1,1,1,1,256,512]{5,4,3,2,1,0:T(8,128)S(1)} all-gather(f32[1,1,1,1,16,512]{5,4,3,2,1,0:T(8,128)S(1)} %get-tuple-element.8), channel_id=2, replica_groups=mesh['layer'=2,'row'=16,'col'=16] {'col'}, dimensions={4}, use_global_device_ids=true | all-gather | bytes 557056 | tf_op jit(solution)/shard_map/all_gather | solution.py:51
  82.5 121.2 %all-gather.27.cloned.1.call-done = f32[4096,512]{1,0:T(8,128)} async-done(((f32[256,512]{1,0:T(8,128)}), f32[4096,512]{1,0:T(8,128)}) %all-gather.27.cloned.1.call-update) | async-done | bytes 8388624 | tf_op jit(solution)/shard_map/all_gather | solution.py:11
  212.2 137.4 %all-reduce.7.cloned.1.call-done = f32[1,256,512]{2,0,1:T(1,128)} async-done(((f32[1,256,512]{2,0,1:T(1,128)}), f32[1,256,512]{2,0,1:T(1,128)}) %all-reduce.7.cloned.1.call-update) | async-done | bytes 524304
  350.4 35.3 %all_gather.82 = f32[1,256,512]{2,0,1:T(1,128)S(1)} all-gather(f32[1,16,512]{2,0,1:T(1,128)S(1)} %fusion.72), channel_id=1, replica_groups=mesh['layer'=2,'row'=16,'col'=16] {'col'}, dimensions={1}, use_global_device_ids=true | all-gather | bytes 557056 | tf_op jit(solution)/shard_map/all_gather | solution.py:51
  386.1 32.3 %all-gather.3 = f32[256,512]{1,0:T(8,128)S(1)} all-gather(f32[16,512]{1,0:T(8,128)S(1)} %bitcast.169), channel_id=5, replica_groups=mesh['layer'=2,'row'=16,'col'=16] {'col'}, dimensions={0}, use_global_device_ids=true | all-gather | bytes 557056 | tf_op jit(solution)/shard_map/all_gather | solution.py:56
  421.5 118.3 %all-gather.29.cloned.1.call-done = f32[4096,512]{1,0:T(8,128)} async-done(((f32[256,512]{1,0:T(8,128)}), f32[4096,512]{1,0:T(8,128)}) %all-gather.29.cloned.1.call-update) | async-done | bytes 8388624 | tf_op jit(solution)/shard_map/all_gather | solution.py:11
  546.4 139.3 %all-reduce.9.cloned.1.call-done = f32[1,256,512]{2,0,1:T(1,128)} async-done(((f32[1,256,512]{2,0,1:T(1,128)}), f32[1,256,512]{2,0,1:T(1,128)}) %all-reduce.9.cloned.1.call-update) | async-done | bytes 524304
  686.5 35.3 %all_gather.86 = f32[1,256,512]{2,0,1:T(1,128)S(1)} all-gather(f32[1,16,512]{2,0,1:T(1,128)S(1)} %fusion.71), channel_id=1, replica_groups=mesh['layer'=2,'row'=16,'col'=16] {'col'}, dimensions={1}, use_global_device_ids=true | all-gather | bytes 557056 | tf_op jit(solution)/shard_map/all_gather | solution.py:51
  761.4 114.6 %all-gather.31.cloned.1.call-done = f32[4096,512]{1,0:T(8,128)} async-done(((f32[256,512]{1,0:T(8,128)}), f32[4096,512]{1,0:T(8,128)}) %all-gather.31.cloned.1.call-update) | async-done | bytes 8388624 | tf_op jit(solution)/shard_map/all_gather | solution.py:11
  883.6 139.3 %all-reduce.11.cloned.1.call-done = f32[1,256,512]{2,0,1:T(1,128)} async-done(((f32[1,256,512]{2,0,1:T(1,128)}), f32[1,256,512]{2,0,1:T(1,128)}) %all-reduce.11.cloned.1.call-update) | async-done | bytes 524304
  1027.1 35.3 %all_gather.90 = f32[1,256,512]{2,0,1:T(1,128)S(1)} all-gather(f32[1,16,512]{2,0,1:T(1,128)S(1)} %reshape_subtract_fusion), channel_id=1, replica_groups=mesh['layer'=2,'row'=16,'col'=16] {'col'}, dimensions={1}, use_global_device_ids=true | all-gather | bytes 557056 | tf_op jit(solution)/shard_map/all_gather | solution.py:51
  1062.8 32.6 %all-gather.7 = f32[256,512]{1,0:T(8,128)S(1)} all-gather(f32[16,512]{1,0:T(8,128)S(1)} %convolution_bitcast_fusion.3), channel_id=9, replica_groups=mesh['layer'=2,'row'=16,'col'=16] {'col'}, dimensions={0}, use_global_device_ids=true | all-gather | bytes 557056 | tf_op jit(solution)/shard_map/all_gather | solution.py:51
  1095.8 34.6 %all-gather.8 = f32[256,512]{1,0:T(8,128)S(1)} all-gather(f32[16,512]{1,0:T(8,128)S(1)} %bitcast.175), channel_id=10, replica_groups=mesh['layer'=2,'row'=16,'col'=16] {'col'}, dimensions={0}, use_global_device_ids=true | all-gather | bytes 557056 | tf_op jit(solution)/shard_map/all_gather | solution.py:56
  1131.9 118.5 %all-gather.33.cloned.1.call-done = f32[4096,512]{1,0:T(8,128)} async-done(((f32[256,512]{1,0:T(8,128)}), f32[4096,512]{1,0:T(8,128)}) %all-gather.33.cloned.1.call-update) | async-done | bytes 8388624 | tf_op jit(solution)/shard_map/all_gather | solution.py:11
  1256.3 71.4 %reduce-scatter.4.cloned.1.call-done = f32[1,16,512]{2,1,0:T(8,128)} async-done(((f32[1,256,512]{2,1,0:T(8,128)}), f32[1,16,512]{2,1,0:T(8,128)}) %reduce-scatter.4.cloned.1.call-update) | async-done | bytes 32784 | tf_op jit(solution)/shard_map/reduce_scatter | solution.py:44
  1328.5 33.8 %all_gather.95 = f32[1,256,512]{2,1,0:T(8,128)S(1)} all-gather(f32[1,16,512]{2,1,0:T(8,128)S(1)} %bitcast_subtract_fusion.1), channel_id=1, replica_groups=mesh['layer'=2,'row'=16,'col'=16] {'col'}, dimensions={1}, use_global_device_ids=true | all-gather | bytes 557056 | tf_op jit(solution)/shard_map/all_gather | solution.py:51
  1362.7 33.3 %all-gather.10 = f32[256,512]{1,0:T(8,128)S(1)} all-gather(f32[16,512]{1,0:T(8,128)S(1)} %bitcast.171), channel_id=12, replica_groups=mesh['layer'=2,'row'=16,'col'=16] {'col'}, dimensions={0}, use_global_device_ids=true | all-gather | bytes 557056 | tf_op jit(solution)/shard_map/all_gather | solution.py:56
  1398.9 117.9 %all-gather.35.cloned.1.call-done = f32[4096,512]{1,0:T(8,128)} async-done(((f32[256,512]{1,0:T(8,128)}), f32[4096,512]{1,0:T(8,128)}) %all-gather.35.cloned.1.call-update) | async-done | bytes 8388624 | tf_op jit(solution)/shard_map/all_gather | solution.py:11
  1522.8 71.4 %reduce-scatter.6.cloned.1.call-done = f32[1,16,512]{2,1,0:T(8,128)} async-done(((f32[1,256,512]{2,1,0:T(8,128)}), f32[1,16,512]{2,1,0:T(8,128)}) %reduce-scatter.6.cloned.1.call-update) | async-done | bytes 32784 | tf_op jit(solution)/shard_map/reduce_scatter | solution.py:44
  1595.0 34.3 %all_gather.99 = f32[1,256,512]{2,1,0:T(8,128)S(1)} all-gather(f32[1,16,512]{2,1,0:T(8,128)S(1)} %bitcast_subtract_fusion), channel_id=1, replica_groups=mesh['layer'=2,'row'=16,'col'=16] {'col'}, dimensions={1}, use_global_device_ids=true | all-gather | bytes 557056 | tf_op jit(solution)/shard_map/all_gather | solution.py:51
  1629.7 32.6 %all-gather.12 = f32[256,512]{1,0:T(8,128)S(1)} all-gather(f32[16,512]{1,0:T(8,128)S(1)} %bitcast.173), channel_id=14, replica_groups=mesh['layer'=2,'row'=16,'col'=16] {'col'}, dimensions={0}, use_global_device_ids=true | all-gather | bytes 557056 | tf_op jit(solution)/shard_map/all_gather | solution.py:56
  1666.5 116.5 %all-gather.37.cloned.1.call-done = f32[4096,512]{1,0:T(8,128)} async-done(((f32[256,512]{1,0:T(8,128)}), f32[4096,512]{1,0:T(8,128)}) %all-gather.37.cloned.1.call-update) | async-done | bytes 8388624 | tf_op jit(solution)/shard_map/all_gather | solution.py:11
  1788.9 71.5 %reduce-scatter.8.cloned.1.call-done = f32[1,16,512]{2,1,0:T(8,128)} async-done(((f32[1,256,512]{2,1,0:T(8,128)}), f32[1,16,512]{2,1,0:T(8,128)}) %reduce-scatter.8.cloned.1.call-update) | async-done | bytes 32784 | tf_op jit(solution)/shard_map/reduce_scatter | solution.py:44
  1861.1 34.0 %all_gather.103 = f32[1,256,512]{2,1,0:T(8,128)S(1)} all-gather(f32[1,16,512]{2,1,0:T(8,128)S(1)} %bitcast_subtract_fusion.2), channel_id=1, replica_groups=mesh['layer'=2,'row'=16,'col'=16] {'col'}, dimensions={1}, use_global_device_ids=true | all-gather | bytes 557056 | tf_op jit(solution)/shard_map/all_gather | solution.py:51
  (91 shorter events, 132.1 us)
Async XLA Ops:
  7.2 1055.2 %copy-start = (f32[1,1,16,256]{3,2,1,0:T(8,128)S(1)}, f32[1,1,16,256]{3,2,1,0:T(8,128)}, u32[]{:S(2)}) copy-start(f32[1,1,16,256]{3,2,1,0:T(8,128)} %param.14) | copy-start | bytes 49156
  7.2 378.5 %copy-start.5 = (f32[1,3,1,1,16,256]{5,4,3,2,1,0:T(8,128)S(1)}, f32[1,3,1,1,16,256]{5,4,3,2,1,0:T(8,128)}, u32[]{:S(2)}) copy-start(f32[1,3,1,1,16,256]{5,4,3,2,1,0:T(8,128)} %param.13) | copy-start | bytes 147460
  7.2 200.9 %copy-start.2 = (f32[1,3,1,1,1,1,256,256]{7,6,5,4,3,2,1,0:T(8,128)S(1)}, f32[1,3,1,1,1,1,256,256]{7,6,5,4,3,2,1,0:T(8,128)}, u32[]{:S(2)}) copy-start(f32[1,3,1,1,1,1,256,256]{7,6,5,4,3,2,1,0:T(8,128)} %param.17) | copy-start | bytes 2359300
  7.2 196.5 %all-gather.27.cloned.1.call-start = ((), (), s32[]{:S(2)}) async-start(), calls=%async_computation.6 | async-start | bytes 8912896 | tf_op jit(solution)/shard_map/all_gather | solution.py:11
  80.2 269.3 %all-reduce.7.cloned.1.call-start = ((), (), s32[]{:S(2)}) async-start(), calls=%async_computation.12 | async-start | bytes 1048576
  210.2 329.6 %all-gather.29.cloned.1.call-start = ((), (), s32[]{:S(2)}) async-start(), calls=%async_computation.7 | async-start | bytes 8912896 | tf_op jit(solution)/shard_map/all_gather | solution.py:11
  419.3 266.4 %all-reduce.9.cloned.1.call-start = ((), (), s32[]{:S(2)}) async-start(), calls=%async_computation.13 | async-start | bytes 1048576
  546.3 329.7 %all-gather.31.cloned.1.call-start = ((), (), s32[]{:S(2)}) async-start(), calls=%async_computation.8 | async-start | bytes 8912896 | tf_op jit(solution)/shard_map/all_gather | solution.py:11
  754.5 272.5 %copy-start.7 = (f32[1,1,16,512]{3,2,1,0:T(8,128)S(1)}, f32[1,1,16,512]{3,2,1,0:T(8,128)}, u32[]{:S(2)}) copy-start(f32[1,1,16,512]{3,2,1,0:T(8,128)} %param.12) | copy-start | bytes 98308
  755.4 267.5 %all-reduce.11.cloned.1.call-start = ((), (), s32[]{:S(2)}) async-start(), calls=%async_computation.14 | async-start | bytes 1048576
  757.5 337.9 %copy-start.8 = (f32[1,1,16,256]{3,2,1,0:T(8,128)S(1)}, f32[1,1,16,256]{3,2,1,0:T(8,128)}, u32[]{:S(2)}) copy-start(f32[1,1,16,256]{3,2,1,0:T(8,128)} %param.16) | copy-start | bytes 49156
  880.4 374.4 %copy-start.1 = (f32[1,3,1,1,1,1,256,256]{7,6,5,4,3,2,1,0:T(8,128)S(1)}, f32[1,3,1,1,1,1,256,256]{7,6,5,4,3,2,1,0:T(8,128)}, u32[]{:S(2)}) copy-start(f32[1,3,1,1,1,1,256,256]{7,6,5,4,3,2,1,0:T(8,128)} %param.20) | copy-start | bytes 2359300
  883.5 478.8 %copy-start.6 = (f32[1,3,1,1,16,256]{5,4,3,2,1,0:T(8,128)S(1)}, f32[1,3,1,1,16,256]{5,4,3,2,1,0:T(8,128)}, u32[]{:S(2)}) copy-start(f32[1,3,1,1,16,256]{5,4,3,2,1,0:T(8,128)} %param.15) | copy-start | bytes 147460
  883.5 366.9 %all-gather.33.cloned.1.call-start = ((), (), s32[]{:S(2)}) async-start(), calls=%async_computation.9 | async-start | bytes 8912896 | tf_op jit(solution)/shard_map/all_gather | solution.py:11
  1095.8 303.1 %copy-start.4 = (f32[512,16]{0,1:T(8,128)}, f32[512,16]{0,1:T(8,128)S(1)}, u32[]{:S(2)}) copy-start(f32[512,16]{0,1:T(8,128)S(1)} %fusion.76) | copy-start | bytes 98308
  1131.3 196.5 %reduce-scatter.4.cloned.1.call-start = ((), (), s32[]{:S(2)}) async-start(), calls=%async_computation.3 | async-start | bytes 557056 | tf_op jit(solution)/shard_map/reduce_scatter | solution.py:44
  1254.8 266.4 %copy-start.3 = (f32[1,3,1,1,1,1,256,256]{7,6,5,4,3,2,1,0:T(8,128)S(1)}, f32[1,3,1,1,1,1,256,256]{7,6,5,4,3,2,1,0:T(8,128)}, u32[]{:S(2)}) copy-start(f32[1,3,1,1,1,1,256,256]{7,6,5,4,3,2,1,0:T(8,128)} %param.19) | copy-start | bytes 2359300
  1256.3 260.5 %all-gather.35.cloned.1.call-start = ((), (), s32[]{:S(2)}) async-start(), calls=%async_computation.10 | async-start | bytes 8912896 | tf_op jit(solution)/shard_map/all_gather | solution.py:11
  1396.9 197.3 %reduce-scatter.6.cloned.1.call-start = ((), (), s32[]{:S(2)}) async-start(), calls=%async_computation.4 | async-start | bytes 557056 | tf_op jit(solution)/shard_map/reduce_scatter | solution.py:44
  1522.7 260.3 %all-gather.37.cloned.1.call-start = ((), (), s32[]{:S(2)}) async-start(), calls=%async_computation.11 | async-start | bytes 8912896 | tf_op jit(solution)/shard_map/all_gather | solution.py:11
  1663.1 197.2 %reduce-scatter.8.cloned.1.call-start = ((), (), s32[]{:S(2)}) async-start(), calls=%async_computation.5 | async-start | bytes 557056 | tf_op jit(solution)/shard_map/reduce_scatter | solution.py:44
Sparse Core Ops, SparseCore 0:
  80.3 123.3 all-gather.26
  210.3 139.1 all-reduce.6
  419.4 120.4 all-gather.28
  546.4 139.2 all-reduce.8
  755.5 120.4 all-gather.30
  883.6 139.2 all-reduce.10
  1131.4 118.9 all-gather.32
  1256.4 71.2 reduce-scatter.3
  1397.0 119.7 all-gather.34
  1522.8 71.3 reduce-scatter.5
  1663.3 119.7 all-gather.36
  1789.0 71.3 reduce-scatter.7
